TPU v7x, 32 devices: a whole 2x2x4 slice. The times are simulated.
32 devices in a mesh: seq: 8 (over z, core), chan: 4 (over y, x).
Axes of the slice: x: 2, y: 2, z: 4, core: 2. Of those that a mesh axis runs over, the one named last changes fastest.
Arguments:
- gate_raw: bfloat16 [8, 2048, 2048], P('seq', None, 'chan'), may hold values from -50 to 50
- value_raw: bfloat16 [8, 2048, 2048], P('seq', None, 'chan'), may hold values from -50 to 50
- filter_gate: float32 [7, 2048], P(None, 'chan'), may hold values from -3 to 3
- filter_value: float32 [7, 2048], P(None, 'chan'), may hold values from -3 to 3
- teacher: float32 [8, 2048, 2048], P('seq', 'chan'), may hold values from -0.25 to 1, as said below
Outputs:
- grad_gate_raw: bfloat16 [8, 2048, 2048], P('seq', None, 'chan')
- grad_value_raw: bfloat16 [8, 2048, 2048], P('seq', None, 'chan')
- grad_filter_gate: float32 [7, 2048], P(None, 'chan')
- grad_filter_value: float32 [7, 2048], P(None, 'chan')
Inputs may be any that keep to these rules, and one draw needn't show every extreme that they name: teacher[s] is symmetric for each of the 8 sequences, with ones on its diagonal.
All inputs are finite; a program needn't handle non-finite values.
Results may differ from a plain program's by a relative error of at most 0.0059.
Values may be sent and summed in bfloat16 or wider, within the bound.
A program may use at most 128 MiB of HBM per device.

v0:
```python
import math
import jax
import jax.numpy as jnp
from jax import lax
from jax.sharding import PartitionSpec as P

TAPS = 7
epsilon = 1e-06


def causal_conv(signal, weights):
    length = signal.shape[1]
    padded = jnp.pad(signal, ((0, 0), (TAPS - 1, 0), (0, 0)))
    summed = jnp.zeros(signal.shape, jnp.float32)
    for tap_index in range(TAPS):
        window = padded[:, TAPS - 1 - tap_index : TAPS - 1 - tap_index + length]
        summed = summed + weights[tap_index] * window.astype(jnp.float32)
    return summed


def adjoint_conv(upstream, weights):
    length = upstream.shape[1]
    padded = jnp.pad(upstream, ((0, 0), (0, TAPS - 1), (0, 0)))
    summed = jnp.zeros(upstream.shape, jnp.float32)
    for tap_index in range(TAPS):
        summed = summed + weights[tap_index] * padded[:, tap_index : tap_index + length]
    return summed


def tap_sums(upstream, signal):
    length = signal.shape[1]
    padded = jnp.pad(signal, ((0, 0), (TAPS - 1, 0), (0, 0)))
    return jnp.stack(
        [
            jnp.sum(
                upstream
                * padded[:, TAPS - 1 - tap_index : TAPS - 1 - tap_index + length].astype(
                    jnp.float32
                ),
                axis=(0, 1),
            )
            for tap_index in range(TAPS)
        ]
    )


def gram_rows(normed, offset, stripe, teacher, factor, full_width):
    own_rows = lax.dynamic_slice_in_dim(normed, offset, stripe, 1)
    similarity = (
        jnp.einsum("srd,std->srt", own_rows, normed, preferred_element_type=jnp.float32)
        / full_width
    )
    residue = (factor * (similarity - teacher)).astype(jnp.bfloat16)
    return jnp.einsum("srt,std->srd", residue, normed, preferred_element_type=jnp.float32)


def on_device(gate_raw, value_raw, filter_gate, filter_value, teacher):
    seq_count, length, local_width = gate_raw.shape
    groups = lax.axis_size("chan")
    stripe = length // groups
    offset = lax.axis_index("chan") * stripe
    full_width = local_width * groups
    factor = 16.0 / math.sqrt(length)
    gate_conv = causal_conv(gate_raw, filter_gate)
    value_conv = causal_conv(value_raw, filter_value)
    hidden = (gate_conv * value_conv).astype(jnp.bfloat16)
    hidden_f = hidden.astype(jnp.float32)
    square_total = lax.psum(jnp.sum(hidden_f * hidden_f, axis=2), "chan")
    inv_rms = lax.rsqrt(square_total[:, :, None] / full_width + epsilon)
    normed_f = hidden_f * inv_rms
    normed = lax.all_gather(normed_f.astype(jnp.bfloat16), "chan", axis=2, tiled=True)
    row_part = gram_rows(normed, offset, stripe, teacher, factor, full_width)
    normed_grad = lax.all_to_all(row_part, "chan", split_axis=2, concat_axis=1, tiled=True)
    projection = lax.psum(jnp.sum(normed_f * normed_grad, axis=2) / full_width, "chan")
    hidden_grad = inv_rms * (normed_grad - normed_f * projection[:, :, None])
    gate_conv_grad = hidden_grad * value_conv
    value_conv_grad = hidden_grad * gate_conv
    grad_gate = adjoint_conv(gate_conv_grad, filter_gate).astype(jnp.bfloat16)
    grad_value = adjoint_conv(value_conv_grad, filter_value).astype(jnp.bfloat16)
    norm_factor = 1.0 / math.sqrt(lax.axis_size("seq") * seq_count * length)
    gate_taps, value_taps = lax.psum(
        (tap_sums(gate_conv_grad, gate_raw), tap_sums(value_conv_grad, value_raw)), "seq"
    )
    return (grad_gate, grad_value, gate_taps * norm_factor, value_taps * norm_factor)


def solution(mesh):
    placed = (
        P("seq", None, "chan"),
        P("seq", None, "chan"),
        P(None, "chan"),
        P(None, "chan"),
        P("seq", "chan", None),
    )
    return jax.shard_map(
        on_device,
        mesh=mesh,
        in_specs=placed,
        out_specs=(
            P("seq", None, "chan"),
            P("seq", None, "chan"),
            P(None, "chan"),
            P(None, "chan"),
        ),
        check_vma=False,
    )
```

profile of v0, /device:TPU:0, one launch (start us, length us, event | category | flops | bytes accessed | tf_op | source)
XLA Modules:
  0.0 296.8 jit_solution(16219476741442778253)
XLA Ops:
  7.2 0.0 all-gather.2.cloned.1.call-start
  7.2 1.0 fusion.66
  8.2 1.0 fusion.65
  9.2 18.7 %fusion.36 = (f32[2048]{0:T(1024)S(1)}, bf16[1,2048,512]{2,1,0:T(8,128)(2,1)S(1)}, f32[1,2048,512]{2,1,0:T(8,128)}, f32[1,2048,512]{2,1,0:T(8,128)}) fusion(f32[512]{0:T(512)S(1)} %bitcast.91, f32[512]{0:T(512)S(1)} %bitcast.93, f32[512]{0:T(512)S(1)} %bitcast.83, f32[512]{0:T(512)S(1)} %bitcast.85, f32[512]{0:T(512)S(1)} %bitcast.87, ...), kind=kLoop, calls=%fused_computation.66 | loop fusion | flops 47183872 | bytes 14716928 | tf_op jit(solution)/shard_map/reduce_sum | solution.py:68
  27.9 11.5 %psum.28 = f32[1,2048]{1,0:T(1,128)S(1)} all-reduce(f32[1,2048]{1,0:T(1,128)S(1)} %bitcast.80), channel_id=1, replica_groups=mesh['seq'=8,'chan'=4] {'chan'}, use_global_device_ids=true, to_apply=%region_1.2 | all-reduce | flops 2048 | bytes 16384 | tf_op jit(solution)/shard_map/psum | solution.py:68
  39.5 1.8 fusion.6
  41.3 0.0 all-gather.2.cloned.1.call-update
  41.3 86.9 %all-gather.2.cloned.1.call-done = bf16[1,2048,2048]{2,1,0:T(8,128)(2,1)} async-done(((bf16[1,2048,512]{2,1,0:T(8,128)(2,1)}), bf16[1,2048,2048]{2,1,0:T(8,128)(2,1)}) %all-gather.2.cloned.1.call-update) | async-done | bytes 8388624 | tf_op jit(solution)/shard_map/all_gather | solution.py:71
  128.1 18.4 %fusion.41 = f32[1,512,2048]{2,1,0:T(8,128)} fusion(bf16[1,2048,2048]{2,1,0:T(8,128)(2,1)} %all-gather.2.cloned.1.call-done, f32[1,512,2048]{2,1,0:T(8,128)} %param.9, s32[]{:T(128)S(6)} %select_n.3), kind=kOutput, calls=%fused_computation.73 | convolution fusion | flops 8594128896 | bytes 27262980 | tf_op jit(solution)/shard_map/srt,std->srd/dot_general | solution.py:54
  146.5 10.9 %copy.10 = f32[1,512,2048]{1,0,2:T(1,128)} copy(f32[1,512,2048]{2,1,0:T(8,128)} %fusion.41) | data formatting | bytes 8388608 | tf_op jit(solution)/shard_map/srt,std->srd/dot_general | solution.py:54
  157.4 53.7 %all_to_all.18 = f32[1,512,2048]{1,0,2:T(1,128)} all-to-all(f32[1,512,2048]{1,0,2:T(1,128)} %copy.10), channel_id=1, replica_groups=mesh['seq'=8,'chan'=4] {'chan'}, dimensions={2} | all-to-all | bytes 8388608 | tf_op jit(solution)/shard_map/all_to_all | solution.py:73
  211.1 10.9 %copy.11 = f32[1,4,512,512]{3,2,1,0:T(8,128)} copy(f32[1,4,512,512]{2,0,3,1:T(1,128)} %bitcast.75) | data formatting | bytes 8388608 | tf_op jit(solution)/shard_map/all_to_all | solution.py:73
  222.0 3.2 %fusion.33 = f32[2048]{0:T(1024)S(1)} fusion(bf16[1,2048,512]{2,1,0:T(8,128)(2,1)S(1)} %get-tuple-element.23, f32[1,4,512,512]{3,2,1,0:T(8,128)} %copy.11, f32[2048]{0:T(1024)S(1)} %bitcast.77), kind=kLoop, calls=%fused_computation.63 | loop fusion | flops 4192256 | bytes 6307840 | tf_op jit(solution)/shard_map/reduce_sum | solution.py:74
  225.2 8.7 %psum.29 = f32[2048]{0:T(1024)S(1)} all-reduce(f32[2048]{0:T(1024)S(1)} %broadcast_multiply_fusion.2), channel_id=1, replica_groups=mesh['seq'=8,'chan'=4] {'chan'}, use_global_device_ids=true, to_apply=%region_3.4 | all-reduce | flops 2048 | bytes 16384 | tf_op jit(solution)/shard_map/psum | solution.py:74
  233.9 0.0 copy-start
  233.9 0.0 copy-start.1
  234.0 0.0 copy-start.2
  234.0 15.5 %fusion.32 = (f32[512]{0:T(512)S(1)}, f32[512]{0:T(512)S(1)}, f32[512]{0:T(512)S(1)}, f32[512]{0:T(512)S(1)}, f32[512]{0:T(512)S(1)}, /*index=5*/f32[512]{0:T(512)S(1)}, f32[512]{0:T(512)S(1)}, f32[1,2048,512]{2,1,0:T(8,128)S(1)}) fusion(bf16[1,2048,512]{2,1,0:T(8,128)(2,1)} %param.6, f32[1,2048,512]{2,1,0:T(8,128)} %get-tuple-element.24, ...), kind=kLoop, calls=%fused_computation.62 | loop fusion | flops 28307968 | bytes 16807936 | tf_op jit(solution)/shard_map/reduce_sum | solution.py:35
  249.5 0.0 copy-done
  249.5 0.0 copy-done.1
  249.5 5.7 %fusion.19 = (f32[512]{0:T(512)S(1)}, f32[512]{0:T(512)S(1)}, f32[512]{0:T(512)S(1)}, f32[512]{0:T(512)S(1)}, f32[512]{0:T(512)S(1)}, /*index=5*/f32[512]{0:T(512)S(1)}, f32[512]{0:T(512)S(1)}, f32[1,2048,512]{2,1,0:T(8,128)S(1)}) fusion(bf16[1,2048,512]{2,1,0:T(8,128)(2,1)S(1)} %copy-done.2, f32[1,2048,512]{2,1,0:T(8,128)S(1)} %copy-done.1, ...), kind=kLoop, calls=%fused_computation.49 | loop fusion | flops 28307968 | bytes 16807936 | tf_op jit(solution)/shard_map/reduce_sum | solution.py:35
  255.2 8.1 %add_convert_fusion = (bf16[1,2048,512]{2,1,0:T(8,128)(2,1)}, bf16[1,2048,512]{2,1,0:T(8,128)(2,1)}) fusion(f32[1,2048,512]{2,1,0:T(8,128)S(1)} %get-tuple-element.20, f32[512]{0:T(512)S(1)} %bitcast.106, f32[512]{0:T(512)S(1)} %bitcast.108, f32[512]{0:T(512)S(1)} %bitcast.98, f32[512]{0:T(512)S(1)} %bitcast.100, f32[512]{0:T(512)S(1)} %bitcast.102, ...), kind=kLoop, calls=%fused_computation.70 | loop fusion | flops 29360128 | bytes 12611584 | tf_op jit(solution)/shard_map/convert_element_type | solution.py:79
  263.4 26.0 %all-reduce.4 = (f32[7,512]{1,0:T(8,128)S(1)}, f32[7,512]{1,0:T(8,128)S(1)}) all-reduce(f32[7,512]{1,0:T(8,128)S(1)} %stack.55, f32[7,512]{1,0:T(8,128)S(1)} %stack.63), channel_id=1, replica_groups=mesh['seq'=8,'chan'=4] {'seq'}, use_global_device_ids=true, to_apply=%region_11.12 | all-reduce | flops 7168 | bytes 57344 | tf_op jit(solution)/shard_map/psum | solution.py:81
  289.4 0.6 broadcast_multiply_fusion
  (5 shorter events, 0.1 us)
Async XLA Ops:
  7.2 121.0 %all-gather.2.cloned.1.call-start = ((), (), s32[]{:S(2)}) async-start(), calls=%async_computation.1 | async-start | bytes 10485760 | tf_op jit(solution)/shard_map/all_gather | solution.py:71
  233.9 15.5 %copy-start = (f32[1,4,512,512]{3,2,1,0:T(8,128)S(1)}, f32[1,4,512,512]{3,2,1,0:T(8,128)}, u32[]{:S(2)}) copy-start(f32[1,4,512,512]{3,2,1,0:T(8,128)} %copy.11) | copy-start | bytes 12582916
  233.9 15.5 %copy-start.1 = (f32[1,2048,512]{2,1,0:T(8,128)S(1)}, f32[1,2048,512]{2,1,0:T(8,128)}, u32[]{:S(2)}) copy-start(f32[1,2048,512]{2,1,0:T(8,128)} %get-tuple-element.25) | copy-start | bytes 12582916
  234.0 15.5 %copy-start.2 = (bf16[1,2048,512]{2,1,0:T(8,128)(2,1)S(1)}, bf16[1,2048,512]{2,1,0:T(8,128)(2,1)}, u32[]{:S(2)}) copy-start(bf16[1,2048,512]{2,1,0:T(8,128)(2,1)} %param.5) | copy-start | bytes 6291460
Sparse Core Ops, SparseCore 0:
  41.4 86.7 all-gather.1
where the time goes:
time: 298 us; the launch traced here: 297 us
  blocking collectives  99.9 us (34%)
  waiting for transfers between devices  86.9 us (29%)
  other arithmetic  53.6 us (18%)
  local copies, waits for them, and re-layouts  23.9 us (8%)
  matrix products  18.4 us (6%)
  between operations  14.1 us (5%)
    all_gather x1, waiting for transfers between devices, on_device(): lax.all_gather(normed_f.astype(jnp.bfloat16), 'chan', axis=2, tiled=True)  86.9 us
    all_to_all x1, blocking collectives, on_device(): lax.all_to_all(row_part, 'chan', split_axis=2, concat_axis=1, tiled=True)  53.7 us
    psum x1, blocking collectives, on_device(): lax.psum((tap_sums(gate_conv_grad, gate_raw), tap_sums(value_conv_grad, v...  26 us
    reduce_sum x2, other arithmetic, tap_sums(): jnp.sum(upstream * padded[:, TAPS - 1 - tap_index:TAPS - 1 - tap_index +...  21.2 us
    reduce_sum x1, other arithmetic, on_device(): square_total = lax.psum(jnp.sum(hidden_f * hidden_f, axis=2), 'chan')  18.7 us
    dot_general x1, matrix products, gram_rows(): jnp.einsum('srt,std->srd', residue, normed, preferred_element_type=jnp.fl...  18.4 us
    psum x1, blocking collectives, on_device(): square_total = lax.psum(jnp.sum(hidden_f * hidden_f, axis=2), 'chan')  11.5 us
    all_to_all x1, local copies, waits for them, and re-layouts, on_device(): lax.all_to_all(row_part, 'chan', split_axis=2, concat_axis=1, tiled=True)  10.9 us
  transfers between devices with their start and end apart: 1, of which 1 were waited for; matrix products, arithmetic and copies ran while one was open for 0% of the time, Pallas kernels for 0%

commit v1 on v0

--- a/solution.py
+++ b/solution.py
@@ -1,3 +1,4 @@
+import functools
 import math
 import jax
 import jax.numpy as jnp
@@ -6,6 +7,17 @@
 
 TAPS = 7
 epsilon = 1e-06
+
+
+def outputs_point(vec, axis_tag, axis_no, axis_k):
+    current_arr = lax.axis_size(axis_tag)
+    response = jnp.split(vec, current_arr, axis=axis_no)
+    wide_out = jnp.stack(response)
+    local_next = lax.all_to_all(wide_out, axis_name=axis_tag, split_axis=0, concat_axis=0)
+    return jnp.concatenate(local_next, axis=axis_k)
+
+
+goods_guide = functools.partial(outputs_point, axis_tag="chan", axis_no=2, axis_k=1)
 
 
 def causal_conv(signal, weights):
@@ -70,7 +82,7 @@
     normed_f = hidden_f * inv_rms
     normed = lax.all_gather(normed_f.astype(jnp.bfloat16), "chan", axis=2, tiled=True)
     row_part = gram_rows(normed, offset, stripe, teacher, factor, full_width)
-    normed_grad = lax.all_to_all(row_part, "chan", split_axis=2, concat_axis=1, tiled=True)
+    normed_grad = goods_guide(row_part)
     projection = lax.psum(jnp.sum(normed_f * normed_grad, axis=2) / full_width, "chan")
     hidden_grad = inv_rms * (normed_grad - normed_f * projection[:, :, None])
     gate_conv_grad = hidden_grad * value_conv

time: 298 us -> 275 us (0.923)
  local copies, waits for them, and re-layouts: 23.9 us -> 6.61 us
  blocking collectives: 99.9 us -> 96.8 us
    all_to_all x1 -> x0, local copies, waits for them, and re-layouts: 10.9 us -> none  [on_device(): lax.all_to_all(row_part, 'chan', split_axis=2, concat_axis=1, tiled=True)]
    dot_general x1 -> x0, local copies, waits for them, and re-layouts: 10.9 us -> none  [gram_rows(): jnp.einsum('srt,std->srd', residue, normed, preferred_element_type=jnp.fl...]
    all_to_all x1, blocking collectives: 53.7 us -> 50.5 us  [outputs_point(): lax.all_to_all(wide_out, axis_name=axis_tag, split_axis=0, concat_axis=0)]
where the time goes in v1:
time: 275 us; the launch traced here: 274 us
  blocking collectives  96.8 us (35%)
  waiting for transfers between devices  86.9 us (32%)
  other arithmetic  51.5 us (19%)
  matrix products  18.4 us (7%)
  between operations  14.2 us (5%)
  local copies, waits for them, and re-layouts  6.61 us (2%)
    all_gather x1, waiting for transfers between devices, on_device(): lax.all_gather(normed_f.astype(jnp.bfloat16), 'chan', axis=2, tiled=True)  86.9 us
    all_to_all x1, blocking collectives, outputs_point(): lax.all_to_all(wide_out, axis_name=axis_tag, split_axis=0, concat_axis=0)  50.5 us
    psum x1, blocking collectives, on_device(): lax.psum((tap_sums(gate_conv_grad, gate_raw), tap_sums(value_conv_grad, v...  26 us
    reduce_sum x2, other arithmetic, tap_sums(): jnp.sum(upstream * padded[:, TAPS - 1 - tap_index:TAPS - 1 - tap_index +...  20.8 us
    reduce_sum x1, other arithmetic, on_device(): square_total = lax.psum(jnp.sum(hidden_f * hidden_f, axis=2), 'chan')  18.7 us
    dot_general x1, matrix products, gram_rows(): jnp.einsum('srt,std->srd', residue, normed, preferred_element_type=jnp.fl...  18.4 us
    psum x1, blocking collectives, on_device(): square_total = lax.psum(jnp.sum(hidden_f * hidden_f, axis=2), 'chan')  11.5 us
    psum x1, blocking collectives, on_device(): lax.psum(jnp.sum(normed_f * normed_grad, axis=2) / full_width, 'chan')  8.74 us
  transfers between devices with their start and end apart: 1, of which 1 were waited for; matrix products, arithmetic and copies ran while one was open for 0% of the time, Pallas kernels for 0%

profile of v1, /device:TPU:0, one launch (start us, length us, event | category | flops | bytes accessed | tf_op | source)
XLA Modules:
  0.0 274.4 jit_solution(15678963234167951332)
XLA Ops:
  7.2 0.0 all-gather.2.cloned.1.call-start
  7.2 1.0 fusion.66
  8.2 1.0 fusion.65
  9.2 18.7 %fusion.36 = (f32[2048]{0:T(1024)S(1)}, bf16[1,2048,512]{2,1,0:T(8,128)(2,1)S(1)}, f32[1,2048,512]{2,1,0:T(8,128)}, f32[1,2048,512]{2,1,0:T(8,128)}) fusion(f32[512]{0:T(512)S(1)} %bitcast.90, f32[512]{0:T(512)S(1)} %bitcast.92, f32[512]{0:T(512)S(1)} %bitcast.82, f32[512]{0:T(512)S(1)} %bitcast.84, f32[512]{0:T(512)S(1)} %bitcast.86, ...), kind=kLoop, calls=%fused_computation.66 | loop fusion | flops 47183872 | bytes 14716928 | tf_op jit(solution)/shard_map/reduce_sum | solution.py:80
  27.9 11.5 %psum.28 = f32[1,2048]{1,0:T(1,128)S(1)} all-reduce(f32[1,2048]{1,0:T(1,128)S(1)} %bitcast.79), channel_id=1, replica_groups=mesh['seq'=8,'chan'=4] {'chan'}, use_global_device_ids=true, to_apply=%region_1.2 | all-reduce | flops 2048 | bytes 16384 | tf_op jit(solution)/shard_map/psum | solution.py:80
  39.5 1.8 fusion.6
  41.3 0.0 all-gather.2.cloned.1.call-update
  41.3 86.9 %all-gather.2.cloned.1.call-done = bf16[1,2048,2048]{2,1,0:T(8,128)(2,1)} async-done(((bf16[1,2048,512]{2,1,0:T(8,128)(2,1)}), bf16[1,2048,2048]{2,1,0:T(8,128)(2,1)}) %all-gather.2.cloned.1.call-update) | async-done | bytes 8388624 | tf_op jit(solution)/shard_map/all_gather | solution.py:83
  128.1 18.4 %fusion.41 = f32[1,512,2048]{2,1,0:T(8,128)} fusion(bf16[1,2048,2048]{2,1,0:T(8,128)(2,1)} %all-gather.2.cloned.1.call-done, f32[1,512,2048]{2,1,0:T(8,128)} %param.9, s32[]{:T(128)S(6)} %select_n.3), kind=kOutput, calls=%fused_computation.74 | convolution fusion | flops 8594128896 | bytes 27262980 | tf_op jit(solution)/shard_map/srt,std->srd/dot_general | solution.py:66
  146.5 2.6 slice_bitcast_fusion.3
  149.2 0.4 pad_maximum_fusion
  149.6 50.5 %all_to_all.5 = f32[4,1,512,512]{3,2,1,0:T(8,128)S(1)} all-to-all(f32[4,1,512,512]{3,2,1,0:T(8,128)S(1)} %pad_maximum_fusion), channel_id=1, replica_groups=mesh['seq'=8,'chan'=4] {'chan'}, dimensions={0} | all-to-all | bytes 8388608 | tf_op jit(solution)/shard_map/all_to_all | solution.py:16
  200.1 1.9 copy-done
  202.1 1.0 fusion.33
  203.1 8.7 %psum.29 = f32[2048]{0:T(1024)S(1)} all-reduce(f32[2048]{0:T(1024)S(1)} %broadcast_multiply_fusion.2), channel_id=1, replica_groups=mesh['seq'=8,'chan'=4] {'chan'}, use_global_device_ids=true, to_apply=%region_3.4 | all-reduce | flops 2048 | bytes 16384 | tf_op jit(solution)/shard_map/psum | solution.py:86
  211.8 0.0 copy-start.1
  211.8 0.0 copy-start.2
  211.8 0.0 copy-start.3
  211.9 15.5 %fusion.32 = (f32[512]{0:T(512)S(1)}, f32[512]{0:T(512)S(1)}, f32[512]{0:T(512)S(1)}, f32[512]{0:T(512)S(1)}, f32[512]{0:T(512)S(1)}, /*index=5*/f32[512]{0:T(512)S(1)}, f32[512]{0:T(512)S(1)}, f32[1,2048,512]{2,1,0:T(8,128)S(1)}) fusion(bf16[1,2048,512]{2,1,0:T(8,128)(2,1)} %param.6, f32[1,2048,512]{2,1,0:T(8,128)} %get-tuple-element.24, ...), kind=kLoop, calls=%fused_computation.62 | loop fusion | flops 28307968 | bytes 16807936 | tf_op jit(solution)/shard_map/reduce_sum | solution.py:47
  227.4 0.0 copy-done.1
  227.4 5.3 %fusion.19 = (f32[512]{0:T(512)S(1)}, f32[512]{0:T(512)S(1)}, f32[512]{0:T(512)S(1)}, f32[512]{0:T(512)S(1)}, f32[512]{0:T(512)S(1)}, /*index=5*/f32[512]{0:T(512)S(1)}, f32[512]{0:T(512)S(1)}, f32[1,2048,512]{2,1,0:T(8,128)S(1)}) fusion(bf16[1,2048,512]{2,1,0:T(8,128)(2,1)S(1)} %copy-done.3, f32[1,2048,512]{2,1,0:T(8,128)S(1)} %copy-done.2, ...), kind=kLoop, calls=%fused_computation.49 | loop fusion | flops 28307968 | bytes 16807936 | tf_op jit(solution)/shard_map/reduce_sum | solution.py:47
  232.7 8.1 %add_convert_fusion = (bf16[1,2048,512]{2,1,0:T(8,128)(2,1)}, bf16[1,2048,512]{2,1,0:T(8,128)(2,1)}) fusion(f32[1,2048,512]{2,1,0:T(8,128)S(1)} %get-tuple-element.20, f32[512]{0:T(512)S(1)} %bitcast.105, f32[512]{0:T(512)S(1)} %bitcast.107, f32[512]{0:T(512)S(1)} %bitcast.97, f32[512]{0:T(512)S(1)} %bitcast.99, f32[512]{0:T(512)S(1)} %bitcast.101, ...), kind=kLoop, calls=%fused_computation.71 | loop fusion | flops 29360128 | bytes 12611584 | tf_op jit(solution)/shard_map/convert_element_type | solution.py:91
  240.9 26.0 %all-reduce.4 = (f32[7,512]{1,0:T(8,128)S(1)}, f32[7,512]{1,0:T(8,128)S(1)}) all-reduce(f32[7,512]{1,0:T(8,128)S(1)} %stack.75, f32[7,512]{1,0:T(8,128)S(1)} %stack.83), channel_id=1, replica_groups=mesh['seq'=8,'chan'=4] {'seq'}, use_global_device_ids=true, to_apply=%region_11.12 | all-reduce | flops 7168 | bytes 57344 | tf_op jit(solution)/shard_map/psum | solution.py:93
  266.9 0.6 broadcast_multiply_fusion
  (7 shorter events, 0.1 us)
Async XLA Ops:
  7.2 121.0 %all-gather.2.cloned.1.call-start = ((), (), s32[]{:S(2)}) async-start(), calls=%async_computation.1 | async-start | bytes 10485760 | tf_op jit(solution)/shard_map/all_gather | solution.py:83
  200.1 1.9 copy-start
  211.8 15.5 %copy-start.1 = (f32[4,1,512,512]{3,2,1,0:T(8,128)S(1)}, f32[4,1,512,512]{3,2,1,0:T(8,128)}, u32[]{:S(2)}) copy-start(f32[4,1,512,512]{3,2,1,0:T(8,128)} %copy-done) | copy-start | bytes 12582916
  211.8 15.5 %copy-start.2 = (f32[1,2048,512]{2,1,0:T(8,128)S(1)}, f32[1,2048,512]{2,1,0:T(8,128)}, u32[]{:S(2)}) copy-start(f32[1,2048,512]{2,1,0:T(8,128)} %get-tuple-element.25) | copy-start | bytes 12582916
  211.8 15.5 %copy-start.3 = (bf16[1,2048,512]{2,1,0:T(8,128)(2,1)S(1)}, bf16[1,2048,512]{2,1,0:T(8,128)(2,1)}, u32[]{:S(2)}) copy-start(bf16[1,2048,512]{2,1,0:T(8,128)(2,1)} %param.5) | copy-start | bytes 6291460
Sparse Core Ops, SparseCore 0:
  41.4 86.7 all-gather.1
